TPU v7x, 32 devices: a whole 2x2x4 slice. The times are simulated.
32 devices in a mesh: dp: 8 (over z, y), mp: 4 (over x, core).
Axes of the slice: x: 2, y: 2, z: 4, core: 2. Of those that a mesh axis runs over, the one named last changes fastest.
Arguments:
- tokens: bfloat16 [192, 196, 768], P('dp'), may hold values from -6 to 6
- cotangent: bfloat16 [192, 196, 768], P('dp'), may hold values from -6 to 6
- counts: int32 [8], replicated, may hold values from 1 to 24, as said below
- vec_params: float32 [5, 768], replicated, as said below
- vec_moments: float32 [2, 5, 768], replicated, as said below
- token_w1: float32 [196, 384], replicated, may hold values from -0.4375 to 0.4375
- token_w1_moments: float32 [2, 196, 384], replicated, as said below
- token_w2: float32 [384, 196], replicated, may hold values from -0.3125 to 0.3125
- token_w2_moments: float32 [2, 384, 196], replicated, as said below
- token_bias: float32 [580], replicated, may hold values from -0.5 to 0.5
- token_bias_moments: float32 [2, 580], replicated, as said below
- chan_w1: float32 [768, 3072], P(None, 'mp'), may hold values from -0.21875 to 0.21875
- chan_w1_moments: float32 [2, 768, 3072], P(None, None, 'mp'), as said below
- chan_b1: float32 [3072], P('mp'), may hold values from -0.5 to 0.5
- chan_b1_moments: float32 [2, 3072], P(None, 'mp'), as said below
- chan_w2: float32 [3072, 768], P('mp'), may hold values from -0.109375 to 0.109375
- chan_w2_moments: float32 [2, 3072, 768], P(None, 'mp'), as said below
Outputs:
- output: bfloat16 [192, 196, 768], P('dp')
- input_grad: bfloat16 [192, 196, 768], P('dp')
- vec_moments_new: float32 [2, 5, 768], replicated
- token_w1_new: float32 [196, 384], replicated
- token_w1_moments_new: float32 [2, 196, 384], replicated
- token_w2_new: float32 [384, 196], replicated
- token_w2_moments_new: float32 [2, 384, 196], replicated
- token_bias_new: float32 [580], replicated
- token_bias_moments_new: float32 [2, 580], replicated
- chan_w1_new: float32 [768, 3072], P(None, 'mp')
- chan_w1_moments_new: float32 [2, 768, 3072], P(None, None, 'mp')
- chan_b1_new: float32 [3072], P('mp')
- chan_b1_moments_new: float32 [2, 3072], P(None, 'mp')
- chan_w2_new: float32 [3072, 768], P('mp')
- chan_w2_moments_new: float32 [2, 3072, 768], P(None, 'mp')
Inputs may be any that keep to these rules, and one draw needn't show every extreme that they name: `counts`: each index of dp holds 1 to 24 live images, the first ones of its slots; some index holds 24. `vec_params`: rows 0 and 2 lie between 0.5 and 1.5. `chan_w1_moments`: the second moments (index 1) are positive. `chan_w2_moments`: the second moments (index 1) are positive. `chan_b1_moments`: the second moments (index 1) are positive. `token_w1_moments`: the second moments (index 1) are positive. `token_w2_moments`: the second moments (index 1) are positive. `token_bias_moments`: the second moments (index 1) are positive. `vec_moments`: the second moments (index 1) are positive.
All inputs are finite; a program needn't handle non-finite values.
Results may differ from a plain program's by a relative error of at most 0.012.
Values may be sent and summed in bfloat16 or wider, within the bound.
No kernel may reach another device: no remote copies, remote signals or barrier semaphores. Data moves between devices by JAX's collectives and lax.ppermute only.
A program may use at most 320 MiB of HBM per device.

v0:
```python
import jax
import jax.numpy as jnp
from jax import lax
from jax.sharding import PartitionSpec as P

STEP = 4
norm_eps = 1e-06
learn_rate = 0.02
decay_rate = 0.5
weight_decay = 0.05
adam_eps = 1e-08


def gelu_exact(values):
    return jax.nn.gelu(values, approximate=False)


def gelu_back(values, grads):
    return jax.vjp(gelu_exact, values)[1](grads)[0]


def norm_parts(values):
    center = values - jnp.mean(values, axis=-1, keepdims=True)
    inv_std = lax.rsqrt(jnp.mean(center * center, axis=-1, keepdims=True) + norm_eps)
    return (center * inv_std, inv_std)


def norm_back(grad_norm, normal, inv_std, gain):
    scaled = grad_norm * gain
    grad_values = inv_std * (
        scaled
        - jnp.mean(scaled, axis=-1, keepdims=True)
        - normal * jnp.mean(scaled * normal, axis=-1, keepdims=True)
    )
    return (grad_values, jnp.sum(grad_norm * normal, axis=(0, 1)), jnp.sum(grad_norm, axis=(0, 1)))


def token_back(token_grad, normed, token_act, token_pre, token_w1_low, token_w2_low):
    token_w2_grad = jnp.einsum(
        "bck,bsc->ks", token_act, token_grad, preferred_element_type=jnp.float32
    )
    out_shift = jnp.sum(token_grad.astype(jnp.float32), axis=(0, 2))
    act_grad = jnp.einsum(
        "bsc,ks->bck", token_grad, token_w2_low, preferred_element_type=jnp.float32
    )
    pre_grad = gelu_back(token_pre, act_grad).astype(jnp.bfloat16)
    token_w1_grad = jnp.einsum("bsc,bck->sk", normed, pre_grad, preferred_element_type=jnp.float32)
    in_shift = jnp.sum(pre_grad.astype(jnp.float32), axis=(0, 1))
    normed_grad = jnp.einsum(
        "bck,sk->bsc", pre_grad, token_w1_low, preferred_element_type=jnp.float32
    )
    return (normed_grad, token_w1_grad, token_w2_grad, jnp.concatenate([in_shift, out_shift]))


def adam_update(weight, moments, grads):
    first = decay_rate * moments[0] + (1.0 - decay_rate) * grads
    second = decay_rate * moments[1] + (1.0 - decay_rate) * grads * grads
    correct = 1.0 - decay_rate**STEP
    step_size = first / correct / (jnp.sqrt(second / correct) + adam_eps)
    return (weight - learn_rate * (step_size + weight_decay * weight), jnp.stack([first, second]))


def new_moments(moments, grads):
    first = decay_rate * moments[0] + (1.0 - decay_rate) * grads
    second = decay_rate * moments[1] + (1.0 - decay_rate) * grads * grads
    return jnp.stack([first, second])


def shards(
    tokens,
    cotangent,
    counts,
    vec_params,
    vec_moments,
    token_w1,
    token_w1_moments,
    token_w2,
    token_w2_moments,
    token_bias,
    token_bias_moments,
    chan_w1,
    chan_w1_moments,
    chan_b1,
    chan_b1_moments,
    chan_w2,
    chan_w2_moments,
):
    images = tokens.shape[0]
    hidden = token_w1.shape[1]
    group_index = lax.axis_index("dp")
    live_count = jnp.sum(jnp.where(jnp.arange(counts.shape[0]) == group_index, counts, 0))
    total = jnp.sum(counts).astype(jnp.float32)
    weight_rows = jnp.where(jnp.arange(images) < live_count, 1.0, 0.0).astype(jnp.float32) / total
    token_w1_low = token_w1.astype(jnp.bfloat16)
    token_w2_low = token_w2.astype(jnp.bfloat16)
    chan_w1_low = chan_w1.astype(jnp.bfloat16)
    chan_w2_low = chan_w2.astype(jnp.bfloat16)
    inputs = tokens.astype(jnp.float32)
    first_norm, first_std = norm_parts(inputs)
    normed = (first_norm * vec_params[0] + vec_params[1]).astype(jnp.bfloat16)
    token_pre = (
        jnp.einsum("bsc,sk->bck", normed, token_w1_low, preferred_element_type=jnp.float32)
        + token_bias[:hidden]
    )
    token_act = gelu_exact(token_pre).astype(jnp.bfloat16)
    token_out = (
        jnp.einsum("bck,ks->bsc", token_act, token_w2_low, preferred_element_type=jnp.float32)
        + token_bias[hidden:][:, None]
    )
    mixed = inputs + token_out
    second_norm, second_std = norm_parts(mixed)
    second = (second_norm * vec_params[2] + vec_params[3]).astype(jnp.bfloat16)
    chan_pre = (
        jnp.einsum("bsc,ch->bsh", second, chan_w1_low, preferred_element_type=jnp.float32) + chan_b1
    )
    chan_act = gelu_exact(chan_pre).astype(jnp.bfloat16)
    partial_out = jnp.einsum(
        "bsh,hc->bsc", chan_act, chan_w2_low, preferred_element_type=jnp.float32
    ).astype(jnp.bfloat16)
    summed = lax.psum(partial_out, "mp").astype(jnp.float32)
    output = (mixed + summed + vec_params[4]).astype(jnp.bfloat16)
    grad_out = cotangent.astype(jnp.float32) * weight_rows[:, None, None]
    grad_low = grad_out.astype(jnp.bfloat16)
    chan_w2_grad = jnp.einsum("bsh,bsc->hc", chan_act, grad_low, preferred_element_type=jnp.float32)
    act_grad = jnp.einsum("bsc,hc->bsh", grad_low, chan_w2_low, preferred_element_type=jnp.float32)
    pre_grad = gelu_back(chan_pre, act_grad).astype(jnp.bfloat16)
    chan_w1_grad = jnp.einsum("bsc,bsh->ch", second, pre_grad, preferred_element_type=jnp.float32)
    chan_b1_grad = jnp.sum(pre_grad.astype(jnp.float32), axis=(0, 1))
    chan_w1_sum, chan_b1_sum, chan_w2_sum = lax.psum(
        (chan_w1_grad, chan_b1_grad, chan_w2_grad), "dp"
    )
    second_part = jnp.einsum(
        "bsh,ch->bsc", pre_grad, chan_w1_low, preferred_element_type=jnp.float32
    )
    second_grad = lax.psum(second_part.astype(jnp.bfloat16), "mp").astype(jnp.float32)
    core_two, gain_two, shift_two = norm_back(second_grad, second_norm, second_std, vec_params[2])
    mixed_grad = grad_out + core_two
    out_shift = jnp.sum(grad_low.astype(jnp.float32), axis=(0, 1))
    token_grad = mixed_grad.astype(jnp.bfloat16)
    normed_grad, token_w1_grad, token_w2_grad, token_bias_grad = token_back(
        token_grad, normed, token_act, token_pre, token_w1_low, token_w2_low
    )
    core_one, gain_one, shift_one = norm_back(normed_grad, first_norm, first_std, vec_params[0])
    input_grad = (mixed_grad + core_one).astype(jnp.bfloat16)
    vec_grad = jnp.stack([gain_one, shift_one, gain_two, shift_two, out_shift])
    vec_sum, token_w1_sum, token_w2_sum, token_bias_sum = lax.psum(
        (vec_grad, token_w1_grad, token_w2_grad, token_bias_grad), "dp"
    )
    vec_moments_new = new_moments(vec_moments, vec_sum)
    token_w1_new, token_w1_moments_new = adam_update(token_w1, token_w1_moments, token_w1_sum)
    token_w2_new, token_w2_moments_new = adam_update(token_w2, token_w2_moments, token_w2_sum)
    token_bias_new, token_bias_moments_new = adam_update(
        token_bias, token_bias_moments, token_bias_sum
    )
    chan_w1_new, chan_w1_moments_new = adam_update(chan_w1, chan_w1_moments, chan_w1_sum)
    chan_b1_new, chan_b1_moments_new = adam_update(chan_b1, chan_b1_moments, chan_b1_sum)
    chan_w2_new, chan_w2_moments_new = adam_update(chan_w2, chan_w2_moments, chan_w2_sum)
    return (
        output,
        input_grad,
        vec_moments_new,
        token_w1_new,
        token_w1_moments_new,
        token_w2_new,
        token_w2_moments_new,
        token_bias_new,
        token_bias_moments_new,
        chan_w1_new,
        chan_w1_moments_new,
        chan_b1_new,
        chan_b1_moments_new,
        chan_w2_new,
        chan_w2_moments_new,
    )


def solution(mesh):
    placed = (
        P("dp", None, None),
        P("dp", None, None),
        P(),
        P(),
        P(),
        P(),
        P(),
        P(),
        P(),
        P(),
        P(),
        P(None, "mp"),
        P(None, None, "mp"),
        P("mp"),
        P(None, "mp"),
        P("mp", None),
        P(None, "mp", None),
    )
    return jax.shard_map(
        shards,
        mesh=mesh,
        in_specs=placed,
        out_specs=(
            P("dp", None, None),
            P("dp", None, None),
            P(),
            P(),
            P(),
            P(),
            P(),
            P(),
            P(),
            P(None, "mp"),
            P(None, None, "mp"),
            P("mp"),
            P(None, "mp"),
            P("mp", None),
            P(None, "mp", None),
        ),
        check_vma=False,
    )
```

profile of v0, /device:TPU:0, one launch (start us, length us, event | category | flops | bytes accessed | tf_op | source)
XLA Modules:
  0.0 795.4 jit_solution(14750361064917613112)
XLA Ops:
  12.1 5.0 convert_reduce_fusion.4
  17.2 7.0 fusion.23
  24.2 24.1 %convert_reduce_fusion.1 = (u32[768,384]{1,0:T(8,128)S(1)}, u32[768,384]{1,0:T(8,128)S(1)}, f32[24,768,384]{2,1,0:T(8,128)}) fusion(f32[384]{0:T(512)S(1)} %slice.67, f32[196,384]{1,0:T(8,128)} %param.22, f32[768]{0:T(1024)S(1)} %get-tuple-element.58, f32[768]{0:T(1024)S(1)} %get-tuple-element.59, f32[24,196]{1,0:T(8,128)S(1)} %add_rsqrt_fusion.1, ...), kind=kOutput, calls=%fused_computation.6 | convolution fusion | flops 2880628224 | bytes 38242560 | tf_op jit(solution)/shard_map/bsc,sk->bck/dot_general | solution.py:102
  48.4 67.2 %multiply_convert_fusion = (bf16[24,768,384]{2,1,0:T(8,128)(2,1)}, f32[24,768,384]{2,1,0:T(8,128)}) fusion(f32[24,768,384]{2,1,0:T(8,128)} %get-tuple-element.110, f32[384]{0:T(512)S(1)} %slice.67, u32[768,384]{1,0:T(8,128)S(1)} %get-tuple-element.46, u32[768,384]{1,0:T(8,128)S(1)} %get-tuple-element.45), kind=kLoop, calls=%fused_computation.9 | loop fusion | flops 488374272 | bytes 73139712 | tf_op jit(solution)/shard_map/convert_element_type | solution.py:105
  115.6 11.3 %fusion.101 = (f32[24,196]{1,0:T(8,128)S(1)}, f32[24,196,768]{2,1,0:T(8,128)S(1)}) fusion(f32[196]{0:T(256)S(1)} %slice.68, bf16[24,768,384]{2,1,0:T(8,128)(2,1)} %get-tuple-element.86, f32[384,196]{0,1:T(8,128)S(1)} %copy-done.7, bf16[24,196,768]{2,0,1:T(8,128)(2,1)} %param.17), kind=kOutput, calls=%fused_computation.194 | convolution fusion | flops 2789053440 | bytes 36152464 | tf_op jit(solution)/shard_map/bck,ks->bsc/dot_general | solution.py:107
  127.0 2.3 multiply_reduce_fusion
  130.3 13.9 %convert_reduce_fusion.6 = (u32[196,768]{1,0:T(8,128)S(1)}, u32[196,768]{1,0:T(8,128)S(1)}, f32[24,196,768]{2,1,0:T(8,128)}) fusion(f32[768]{0:T(1024)S(1)} %copy-done.18, f32[768,768]{1,0:T(8,128)S(1)} %copy-done.2, f32[24,196,768]{2,1,0:T(8,128)S(1)} %get-tuple-element.112, f32[768]{0:T(1024)S(1)} %get-tuple-element.60, f32[768]{0:T(1024)S(1)} %get-tuple-element.57, ...), kind=kOutput, calls=%fused_computation.57 | convolution fusion | flops 5610768384 | bytes 32511744 | tf_op jit(solution)/shard_map/bsc,ch->bsh/dot_general | solution.py:114
  144.2 36.2 %multiply_convert_fusion.1 = (bf16[24,196,768]{2,1,0:T(8,128)(2,1)S(1)}, f32[24,196,768]{2,1,0:T(8,128)}) fusion(f32[24,196,768]{2,1,0:T(8,128)} %get-tuple-element.113, f32[768]{0:T(1024)S(1)} %copy-done.18, u32[196,768]{1,0:T(8,128)S(1)} %get-tuple-element.53, u32[196,768]{1,0:T(8,128)S(1)} %get-tuple-element.52), kind=kLoop, calls=%fused_computation.66 | loop fusion | flops 249274368 | bytes 37334016 | tf_op jit(solution)/shard_map/convert_element_type | solution.py:116
  180.4 26.0 %convert_reduce_fusion.7 = (f32[768]{0:T(1024)}, bf16[24,196,768]{2,1,0:T(8,128)(2,1)}) fusion(f32[24,196,768]{2,1,0:T(8,128)} %get-tuple-element.85, f32[768,768]{1,0:T(8,128)S(1)} %copy-done.4, f32[24]{0:T(128)S(1)} %fusion.88, bf16[24,196,768]{2,0,1:T(8,128)(2,1)} %param.18, f32[24,196,768]{2,1,0:T(8,128)} %get-tuple-element.113, f32[768]{0:T(1024)S(1)} %copy-done.18), kind=kOutput, calls=%fused_computation.59 | convolution fusion | flops 5621906432 | bytes 45717600 | tf_op jit(solution)/shard_map/bsc,hc->bsh/dot_general | solution.py:125
  206.4 11.2 %convolution_convert_fusion = bf16[24,196,768]{2,1,0:T(8,128)(2,1)} fusion(bf16[24,196,768]{2,1,0:T(8,128)(2,1)} %get-tuple-element.118, f32[768,768]{1,0:T(8,128)S(1)} %copy-done.3), kind=kOutput, calls=%fused_computation.83 | convolution fusion | flops 5553266688 | bytes 16809984 | tf_op jit(solution)/shard_map/bsh,ch->bsc/dot_general | solution.py:132
  217.6 8.0 %convolution_convert_fusion.1 = bf16[24,196,768]{2,1,0:T(8,128)(2,1)} fusion(bf16[24,196,768]{2,1,0:T(8,128)(2,1)S(1)} %get-tuple-element.84, f32[768,768]{1,0:T(8,128)S(1)} %copy-done.4), kind=kOutput, calls=%fused_computation.84 | convolution fusion | flops 5553266688 | bytes 16809984 | tf_op jit(solution)/shard_map/bsh,hc->bsc/dot_general | solution.py:117
  230.7 14.2 %convolution_bitcast_fusion = f32[768,768]{1,0:T(8,128)} fusion(bf16[24,196,768]{2,1,0:T(8,128)(2,1)} %copy-done.1, f32[24]{0:T(128)S(1)} %fusion.88, bf16[24,196,768]{2,0,1:T(8,128)(2,1)} %param.18), kind=kOutput, calls=%fused_computation.99 | convolution fusion | flops 5559902208 | bytes 16810080 | tf_op jit(solution)/shard_map/bsh,bsc->hc/dot_general | solution.py:124
  245.0 12.1 %convolution_bitcast_fusion.1 = f32[768,768]{1,0:T(8,128)} fusion(bf16[24,196,768]{2,1,0:T(8,128)(2,1)} %get-tuple-element.118, f32[24,196,768]{2,1,0:T(8,128)S(1)} %bitcast.144, f32[768]{0:T(1024)S(1)} %get-tuple-element.60, f32[768]{0:T(1024)S(1)} %get-tuple-element.57, f32[24,196]{1,0:T(8,128)S(1)} %add_rsqrt_fusion, ...), kind=kOutput, calls=%fused_computation.100 | convolution fusion | flops 5567127552 | bytes 24079104 | tf_op jit(solution)/shard_map/bsc,bsh->ch/dot_general | solution.py:127
  257.1 227.4 %all-reduce.8.cloned.1.call-done = (bf16[24,196,768]{2,1,0:T(8,128)(2,1)}, bf16[24,196,768]{2,1,0:T(8,128)(2,1)}) async-done(((bf16[24,196,768]{2,1,0:T(8,128)(2,1)}, bf16[24,196,768]{2,1,0:T(8,128)(2,1)}), (bf16[24,196,768]{2,1,0:T(8,128)(2,1)}, bf16[24,196,768]{2,1,0:T(8,128)(2,1)})) %all-reduce.8.cloned.1.call-update) | async-done | bytes 14450704 | tf_op jit(solution)/shard_map/psum | solution.py:120
  484.5 12.4 %fusion.29 = (f32[768]{0:T(1024)S(1)}, f32[24,196]{1,0:T(8,128)S(1)}, f32[24,196]{1,0:T(8,128)S(1)}, f32[768]{0:T(1024)S(1)}) fusion(bf16[24,196,768]{2,1,0:T(8,128)(2,1)} %get-tuple-element.75, f32[24,196,768]{2,1,0:T(8,128)} %copy-done, f32[24,196]{1,0:T(8,128)S(1)} %add_rsqrt_fusion, f32[24,196]{1,0:T(8,128)S(1)} %broadcast_multiply_fusion.4, ...), kind=kLoop, calls=%fused_computation.52 | loop fusion | flops 36115776 | bytes 21760512 | tf_op jit(solution)/shard_map/reduce_sum | solution.py:35
  497.0 24.4 %convert_reduce_fusion.8 = (f32[196]{0:T(256)}, f32[24,196,768]{2,1,0:T(8,128)}, bf16[24,196,768]{2,1,0:T(8,128)(2,1)}, f32[768]{0:T(1024)S(1)}) fusion(f32[24,196]{1,0:T(8,128)S(1)} %get-tuple-element.119, f32[24,196,768]{2,1,0:T(8,128)} %copy-done, f32[24,196]{1,0:T(8,128)S(1)} %broadcast_multiply_fusion.4, f32[24,196]{1,0:T(8,128)S(1)} %get-tuple-element.120, ...), kind=kLoop, calls=%fused_computation.60 | loop fusion | flops 75865152 | bytes 57888112 | tf_op jit(solution)/shard_map/reduce_sum | solution.py:42
  521.4 13.9 %convolution_bitcast_fusion.2 = f32[384,196]{0,1:T(8,128)} fusion(bf16[24,768,384]{2,1,0:T(8,128)(2,1)} %get-tuple-element.86, f32[24,196,768]{2,1,0:T(8,128)} %get-tuple-element.83), kind=kOutput, calls=%fused_computation.102 | convolution fusion | flops 2778144768 | bytes 28907520 | tf_op jit(solution)/shard_map/bck,bsc->ks/dot_general | solution.py:39
  535.4 30.6 %convert_reduce_fusion.2 = (f32[384]{0:T(512)}, bf16[24,768,384]{2,1,0:T(8,128)(2,1)}) fusion(f32[24,768,384]{2,1,0:T(8,128)} %get-tuple-element.87, f32[384,196]{0,1:T(8,128)S(1)} %copy-done.8, f32[24,196,768]{2,1,0:T(8,128)} %get-tuple-element.83, f32[24,768,384]{2,1,0:T(8,128)} %get-tuple-element.110, f32[384]{0:T(512)S(1)} %copy-done.24), kind=kOutput, calls=%fused_computation.7 | convolution fusion | flops 2898543616 | bytes 85533696 | tf_op jit(solution)/shard_map/bsc,ks->bck/dot_general | solution.py:43
  566.0 11.7 %fusion.45 = f32[196,384]{1,0:T(8,128)} fusion(bf16[24,768,384]{2,1,0:T(8,128)(2,1)} %get-tuple-element.116, f32[768]{0:T(1024)S(1)} %copy-done.28, f32[768]{0:T(1024)S(1)} %copy-done.21, f32[24,196]{1,0:T(8,128)S(1)} %copy-done.15, f32[24,196]{1,0:T(8,128)S(1)} %copy-done.13, bf16[24,196,768]{2,0,1:T(8,128)(2,1)} %param.17), kind=kOutput, calls=%fused_computation.101 | convolution fusion | flops 2796208128 | bytes 21725952 | tf_op jit(solution)/shard_map/bsc,bck->sk/dot_general | solution.py:47
  577.7 19.0 %fusion.22 = (f32[768]{0:T(1024)S(1)}, f32[24,196]{1,0:T(8,128)}, f32[24,196]{1,0:T(8,128)}, f32[24,768,196]{1,2,0:T(8,128)}) fusion(f32[24,196]{1,0:T(8,128)S(1)} %copy-done.15, f32[24,196]{1,0:T(8,128)S(1)} %copy-done.13, bf16[24,196,768]{2,0,1:T(8,128)(2,1)} %param.17, f32[768]{0:T(1024)S(1)} %copy-done.21, ...), kind=kOutput, calls=%fused_computation.45 | convolution fusion | flops 2807111424 | bytes 36214272 | tf_op jit(solution)/shard_map/bck,sk->bsc/dot_general | solution.py:49
  599.0 6.2 reduce_sum.173
  607.8 40.4 %all-reduce = (f32[5,768]{1,0:T(8,128)}, f32[580]{0:T(1024)}, f32[768]{0:T(1024)}) all-reduce(f32[5,768]{1,0:T(8,128)S(1)} %stack.86, f32[580]{0:T(1024)} %pad_maximum_fusion.7, f32[768]{0:T(1024)} %get-tuple-element.117), channel_id=1, replica_groups=mesh['dp'=8,'mp'=4] {'dp'}, use_global_device_ids=true, to_apply=%region_17.18 | all-reduce | flops 5188 | bytes 41504 | tf_op jit(solution)/shard_map/psum | solution.py:146
  653.8 16.5 %fusion.21 = bf16[24,196,768]{2,1,0:T(8,128)(2,1)} fusion(f32[24,196,768]{2,1,0:T(8,128)} %get-tuple-element.83, f32[24,768,196]{1,2,0:T(8,128)} %get-tuple-element.114, f32[24,196]{1,0:T(8,128)S(1)} %broadcast_multiply_fusion, f32[24,196]{1,0:T(8,128)S(1)} %broadcast_multiply_fusion.1, f32[768]{0:T(1024)} %copy-done.20, f32[24,196]{1,0:T(8,128)} %copy-done.14, ...), kind=kLoop, calls=%fused_computation.44 | loop fusion | flops 36126720 | bytes 43430400 | tf_op jit(solution)/shard_map/convert_element_type | solution.py:144
  670.3 7.6 copy.54
  677.9 4.4 copy.53
  683.5 82.9 %all-reduce.6.cloned.1.call-done = (f32[196,384]{1,0:T(8,128)}, f32[384,196]{0,1:T(8,128)}, f32[768,768]{1,0:T(8,128)}, f32[768,768]{1,0:T(8,128)}) async-done(((f32[196,384]{1,0:T(8,128)}, f32[384,196]{0,1:T(8,128)}, f32[768,768]{1,0:T(8,128)}, f32[768,768]{1,0:T(8,128)}), (f32[196,384]{1,0:T(8,128)}, f32[384,196]{0,1:T(8,128)}, f32[768,768]{1,0:T(8,128)}, ...) | async-done | bytes 5320720 | tf_op jit(solution)/shard_map/psum | solution.py:146
  766.5 2.2 fusion.72
  769.9 2.2 fusion.73
  773.3 6.9 fusion.53
  780.2 2.5 pad_maximum_fusion
  782.7 3.1 fusion.54
  785.8 2.5 pad_maximum_fusion.1
  (130 shorter events, 24.7 us)
Async XLA Ops:
  7.2 477.3 %all-reduce.8.cloned.1.call-start = ((), (), s32[]{:S(2)}) async-start(), calls=%async_computation.1 | async-start | bytes 29491200 | tf_op jit(solution)/shard_map/psum | solution.py:120
  8.6 39.8 %copy-start.23 = (f32[384]{0:T(512)}, f32[384]{0:T(512)S(1)}, u32[]{:S(2)}) copy-start(f32[384]{0:T(512)S(1)} %slice.67) | copy-start | bytes 4612
  12.1 36.2 %copy-start.20 = (f32[768]{0:T(1024)}, f32[768]{0:T(1024)S(1)}, u32[]{:S(2)}) copy-start(f32[768]{0:T(1024)S(1)} %get-tuple-element.59) | copy-start | bytes 9220
  12.1 36.2 %copy-start.27 = (f32[768]{0:T(1024)}, f32[768]{0:T(1024)S(1)}, u32[]{:S(2)}) copy-start(f32[768]{0:T(1024)S(1)} %get-tuple-element.58) | copy-start | bytes 9220
  17.2 31.2 %copy-start.12 = (f32[24,196]{1,0:T(8,128)}, f32[24,196]{1,0:T(8,128)S(1)}, u32[]{:S(2)}) copy-start(f32[24,196]{1,0:T(8,128)S(1)} %broadcast_multiply_fusion.5) | copy-start | bytes 56452
  24.2 24.2 %copy-start.14 = (f32[24,196]{1,0:T(8,128)}, f32[24,196]{1,0:T(8,128)S(1)}, u32[]{:S(2)}) copy-start(f32[24,196]{1,0:T(8,128)S(1)} %add_rsqrt_fusion.1) | copy-start | bytes 56452
  48.4 67.2 %copy-start.7 = (f32[384,196]{0,1:T(8,128)S(1)}, f32[384,196]{0,1:T(8,128)}, u32[]{:S(2)}) copy-start(f32[384,196]{0,1:T(8,128)} %param.24) | copy-start | bytes 903172
  126.9 17.3 %copy-start = (f32[24,196,768]{2,1,0:T(8,128)}, f32[24,196,768]{2,1,0:T(8,128)S(1)}, u32[]{:S(2)}) copy-start(f32[24,196,768]{2,1,0:T(8,128)S(1)} %get-tuple-element.112) | copy-start | bytes 43352068
  144.2 36.2 %copy-start.4 = (f32[768,768]{1,0:T(8,128)S(1)}, f32[768,768]{1,0:T(8,128)}, u32[]{:S(2)}) copy-start(f32[768,768]{1,0:T(8,128)} %param.32) | copy-start | bytes 7077892
  180.4 37.2 %copy-start.1 = (bf16[24,196,768]{2,1,0:T(8,128)(2,1)}, bf16[24,196,768]{2,1,0:T(8,128)(2,1)S(1)}, u32[]{:S(2)}) copy-start(bf16[24,196,768]{2,1,0:T(8,128)(2,1)S(1)} %get-tuple-element.84) | copy-start | bytes 21676036
  180.4 26.0 %copy-start.3 = (f32[768,768]{1,0:T(8,128)S(1)}, f32[768,768]{1,0:T(8,128)}, u32[]{:S(2)}) copy-start(f32[768,768]{1,0:T(8,128)} %param.28) | copy-start | bytes 7077892
  225.7 540.8 %all-reduce.6.cloned.1.call-start = ((), (), s32[]{:S(2)}) async-start(), calls=%async_computation | async-start | bytes 10665984 | tf_op jit(solution)/shard_map/psum | solution.py:146
  229.4 15.5 %slice-start = ((s8[14745600]{0:T(1024)(128)(4,1)}), s8[4194304]{0:T(1024)(128)(4,1)S(1)}, s32[]{:S(2)}) async-start(s8[14745600]{0:T(1024)(128)(4,1)} %bitcast.143), calls=%async_computation.2 | async-start | bytes 8388608
  230.7 14.3 %slice-start.1 = ((s8[14745600]{0:T(1024)(128)(4,1)}), s8[4194304]{0:T(1024)(128)(4,1)S(1)}, s32[]{:S(2)}) async-start(s8[14745600]{0:T(1024)(128)(4,1)} %bitcast.143), calls=%async_computation.3 | async-start | bytes 8388608
  230.7 14.3 %slice-start.2 = ((s8[14745600]{0:T(1024)(128)(4,1)}), s8[4194304]{0:T(1024)(128)(4,1)S(1)}, s32[]{:S(2)}) async-start(s8[14745600]{0:T(1024)(128)(4,1)} %bitcast.143), calls=%async_computation.4 | async-start | bytes 8388608
  230.7 14.3 %slice-start.3 = ((s8[14745600]{0:T(1024)(128)(4,1)}), s8[2162688]{0:T(1024)(128)(4,1)S(1)}, s32[]{:S(2)}) async-start(s8[14745600]{0:T(1024)(128)(4,1)} %bitcast.143), calls=%async_computation.5 | async-start | bytes 4325376
  257.1 239.9 %copy-start.22 = (f32[768]{0:T(1024)S(1)}, f32[768]{0:T(1024)}, u32[]{:S(2)}) copy-start(f32[768]{0:T(1024)} %get-tuple-element.56) | copy-start | bytes 9220
  484.5 12.5 %slice-start.7 = ((s8[7372800]{0:T(1024)(128)(4,1)}), s8[3178496]{0:T(1024)(128)(4,1)S(1)}, s32[]{:S(2)}) async-start(s8[7372800]{0:T(1024)(128)(4,1)} %bitcast.147), calls=%async_computation.9 | async-start | bytes 6356992
  484.5 12.5 %slice-start.9 = ((s8[7372800]{0:T(1024)(128)(4,1)}), s8[3178496]{0:T(1024)(128)(4,1)S(1)}, s32[]{:S(2)}) async-start(s8[7372800]{0:T(1024)(128)(4,1)} %bitcast.149), calls=%async_computation.11 | async-start | bytes 6356992
  521.4 13.9 %copy-start.8 = (f32[384,196]{0,1:T(8,128)S(1)}, f32[384,196]{0,1:T(8,128)}, u32[]{:S(2)}) copy-start(f32[384,196]{0,1:T(8,128)} %param.24) | copy-start | bytes 903172
  521.4 13.9 %copy-start.24 = (f32[384]{0:T(512)S(1)}, f32[384]{0:T(512)}, u32[]{:S(2)}) copy-start(f32[384]{0:T(512)} %copy-done.23) | copy-start | bytes 4612
  535.3 30.6 %copy-start.13 = (f32[24,196]{1,0:T(8,128)S(1)}, f32[24,196]{1,0:T(8,128)}, u32[]{:S(2)}) copy-start(f32[24,196]{1,0:T(8,128)} %copy-done.12) | copy-start | bytes 56452
  535.3 30.6 %copy-start.15 = (f32[24,196]{1,0:T(8,128)S(1)}, f32[24,196]{1,0:T(8,128)}, u32[]{:S(2)}) copy-start(f32[24,196]{1,0:T(8,128)} %copy-done.14) | copy-start | bytes 56452
  535.3 30.6 %copy-start.21 = (f32[768]{0:T(1024)S(1)}, f32[768]{0:T(1024)}, u32[]{:S(2)}) copy-start(f32[768]{0:T(1024)} %copy-done.20) | copy-start | bytes 9220
  535.4 30.6 %copy-start.28 = (f32[768]{0:T(1024)S(1)}, f32[768]{0:T(1024)}, u32[]{:S(2)}) copy-start(f32[768]{0:T(1024)} %copy-done.27) | copy-start | bytes 9220
  596.7 51.6 %copy-start.16 = (f32[1,5,768]{2,0,1:T(1,128)S(1)}, f32[1,5,768]{2,0,1:T(1,128)}, u32[]{:S(2)}) copy-start(f32[1,5,768]{2,0,1:T(1,128)} %get-tuple-element.106) | copy-start | bytes 46084
  596.7 54.3 %copy-start.19 = (f32[768]{0:T(1024)S(1)}, f32[768]{0:T(1024)}, u32[]{:S(2)}) copy-start(f32[768]{0:T(1024)} %param.30) | copy-start | bytes 9220
  599.0 78.9 %slice-start.4 = ((s8[7372800]{0:T(1024)(128)(4,1)}), s8[3178496]{0:T(1024)(128)(4,1)S(1)}, s32[]{:S(2)}) async-start(s8[7372800]{0:T(1024)(128)(4,1)} %bitcast.145), calls=%async_computation.6 | async-start | bytes 6356992
  653.8 24.1 %slice-start.5 = ((s8[7372800]{0:T(1024)(128)(4,1)}), s8[4194304]{0:T(1024)(128)(4,1)S(1)}, s32[]{:S(2)}) async-start(s8[7372800]{0:T(1024)(128)(4,1)} %bitcast.145), calls=%async_computation.7 | async-start | bytes 8388608
  769.9 12.8 %slice-start.10 = ((s8[4718592]{0:T(1024)(128)(4,1)}), s8[4194304]{0:T(1024)(128)(4,1)S(1)}, s32[]{:S(2)}) async-start(s8[4718592]{0:T(1024)(128)(4,1)} %bitcast.151), calls=%async_computation.12 | async-start | bytes 8388608
  769.9 12.8 %copy-start.5 = (f32[768,768]{1,0:T(8,128)S(1)}, f32[768,768]{1,0:T(8,128)}, u32[]{:S(2)}) copy-start(f32[768,768]{1,0:T(8,128)} %param.32) | copy-start | bytes 7077892
  769.9 12.8 %copy-start.6 = (f32[768,768]{1,0:T(8,128)S(1)}, f32[768,768]{1,0:T(8,128)}, u32[]{:S(2)}) copy-start(f32[768,768]{1,0:T(8,128)} %get-tuple-element.73) | copy-start | bytes 7077892
  (11 other events, 63.1 us)
Sparse Core Ops, SparseCore 0:
  225.8 258.6 all-reduce.7
  577.8 188.6 all-reduce.5
where the time goes:
time: 799 us; the launch traced here: 795 us
  waiting for transfers between devices  310 us (39%)
  other arithmetic  208 us (26%)
  matrix products  196 us (25%)
  blocking collectives  40.4 us (5%)
  local copies, waits for them, and re-layouts  25.7 us (3%)
  between operations  15.3 us (2%)
    psum x1, waiting for transfers between devices, shards(): summed = lax.psum(partial_out, 'mp').astype(jnp.float32)  227 us
    psum x1, waiting for transfers between devices, shards(): lax.psum((vec_grad, token_w1_grad, token_w2_grad, token_bias_grad), 'dp')  82.9 us
    convert_element_type x1, other arithmetic, shards(): token_act = gelu_exact(token_pre).astype(jnp.bfloat16)  67.2 us
    psum x1, blocking collectives, shards(): lax.psum((vec_grad, token_w1_grad, token_w2_grad, token_bias_grad), 'dp')  40.4 us
    convert_element_type x1, other arithmetic, shards(): chan_act = gelu_exact(chan_pre).astype(jnp.bfloat16)  36.2 us
    dot_general x1, matrix products, token_back(): jnp.einsum('bsc,ks->bck', token_grad, token_w2_low, preferred_element_typ...  30.6 us
    dot_general x1, matrix products, shards(): jnp.einsum('bsc,hc->bsh', grad_low, chan_w2_low, preferred_element_type=j...  26 us
    reduce_sum x1, other arithmetic, token_back(): out_shift = jnp.sum(token_grad.astype(jnp.float32), axis=(0, 2))  24.4 us
  transfers between devices with their start and end apart: 2, of which 2 were waited for; matrix products, arithmetic and copies ran while one was open for 12% of the time, Pallas kernels for 0%

commit v1 on v0

--- a/solution.py
+++ b/solution.py
@@ -1,3 +1,4 @@
+import functools
 import jax
 import jax.numpy as jnp
 from jax import lax
@@ -9,6 +10,14 @@
 decay_rate = 0.5
 weight_decay = 0.05
 adam_eps = 1e-08
+
+
+def _wrap_pipes(arr_in, group_axis):
+    view_out = jnp.sum(lax.all_gather(arr_in, group_axis), 0)
+    return view_out
+
+
+_replace_counts = functools.partial(_wrap_pipes, group_axis="mp")
 
 
 def gelu_exact(values):
@@ -117,7 +126,7 @@
     partial_out = jnp.einsum(
         "bsh,hc->bsc", chan_act, chan_w2_low, preferred_element_type=jnp.float32
     ).astype(jnp.bfloat16)
-    summed = lax.psum(partial_out, "mp").astype(jnp.float32)
+    summed = _replace_counts(partial_out).astype(jnp.float32)
     output = (mixed + summed + vec_params[4]).astype(jnp.bfloat16)
     grad_out = cotangent.astype(jnp.float32) * weight_rows[:, None, None]
     grad_low = grad_out.astype(jnp.bfloat16)

time: 799 us -> 847 us (1.060)
  waiting for transfers between devices: 310 us -> 345 us
  other arithmetic: 208 us -> 222 us
    all_gather x0 -> x1, waiting for transfers between devices: none -> 165 us  [_wrap_pipes(): view_out = jnp.sum(lax.all_gather(arr_in, group_axis), 0)]
    psum x1, waiting for transfers between devices: 227 us -> 96.3 us  [shards(): lax.psum(second_part.astype(jnp.bfloat16), 'mp').astype(jnp.float32)]
    reduce_sum x0 -> x1, other arithmetic: none -> 14.5 us  [_wrap_pipes(): view_out = jnp.sum(lax.all_gather(arr_in, group_axis), 0)]
    unnamed x87 -> x79, local copies, waits for them, and re-layouts: 15.9 us -> 18.3 us
  transfers between devices with their start and end apart: 2 -> 3, of which waited for: 2 -> 3; matrix products, arithmetic and copies ran while one was open for 12% -> 14% of each run, Pallas kernels for 0% -> 0%
where the time goes in v1:
time: 847 us; the launch traced here: 844 us
  waiting for transfers between devices  345 us (41%)
  other arithmetic  222 us (26%)
  matrix products  188 us (22%)
  blocking collectives  40.7 us (5%)
  local copies, waits for them, and re-layouts  32.5 us (4%)
  between operations  15 us (2%)
    all_gather x1, waiting for transfers between devices, _wrap_pipes(): view_out = jnp.sum(lax.all_gather(arr_in, group_axis), 0)  165 us
    psum x1, waiting for transfers between devices, shards(): lax.psum(second_part.astype(jnp.bfloat16), 'mp').astype(jnp.float32)  96.3 us
    psum x1, waiting for transfers between devices, shards(): lax.psum((vec_grad, token_w1_grad, token_w2_grad, token_bias_grad), 'dp')  83.8 us
    convert_element_type x1, other arithmetic, shards(): token_act = gelu_exact(token_pre).astype(jnp.bfloat16)  67.2 us
    psum x1, blocking collectives, shards(): lax.psum((vec_grad, token_w1_grad, token_w2_grad, token_bias_grad), 'dp')  40.7 us
    convert_element_type x1, other arithmetic, shards(): chan_act = gelu_exact(chan_pre).astype(jnp.bfloat16)  36.3 us
    dot_general x1, matrix products, token_back(): jnp.einsum('bsc,ks->bck', token_grad, token_w2_low, preferred_element_typ...  30.6 us
    reduce_sum x1, other arithmetic, token_back(): out_shift = jnp.sum(token_grad.astype(jnp.float32), axis=(0, 2))  24.5 us
  transfers between devices with their start and end apart: 3, of which 3 were waited for; matrix products, arithmetic and copies ran while one was open for 14% of the time, Pallas kernels for 0%

profile of v1, /device:TPU:0, one launch (start us, length us, event | category | flops | bytes accessed | tf_op | source)
XLA Modules:
  0.0 843.9 jit_solution(2870631457323520814)
XLA Ops:
  12.1 5.0 convert_reduce_fusion.4
  17.2 7.0 fusion.23
  24.2 23.9 %convert_reduce_fusion.1 = (u32[768,384]{1,0:T(8,128)S(1)}, u32[768,384]{1,0:T(8,128)S(1)}, f32[24,768,384]{2,1,0:T(8,128)}) fusion(f32[384]{0:T(512)S(1)} %slice.67, f32[196,384]{1,0:T(8,128)} %param.22, f32[768]{0:T(1024)S(1)} %get-tuple-element.88, f32[768]{0:T(1024)S(1)} %get-tuple-element.89, f32[24,196]{1,0:T(8,128)S(1)} %add_rsqrt_fusion.1, ...), kind=kOutput, calls=%fused_computation.6 | convolution fusion | flops 2880628224 | bytes 38242560 | tf_op jit(solution)/shard_map/bsc,sk->bck/dot_general | solution.py:111
  48.2 67.2 %multiply_convert_fusion = (bf16[24,768,384]{2,1,0:T(8,128)(2,1)}, f32[24,768,384]{2,1,0:T(8,128)}) fusion(f32[24,768,384]{2,1,0:T(8,128)} %get-tuple-element.138, f32[384]{0:T(512)S(1)} %slice.67, u32[768,384]{1,0:T(8,128)S(1)} %get-tuple-element.76, u32[768,384]{1,0:T(8,128)S(1)} %get-tuple-element.75), kind=kLoop, calls=%fused_computation.9 | loop fusion | flops 488374272 | bytes 73139712 | tf_op jit(solution)/shard_map/convert_element_type | solution.py:114
  115.4 11.3 %fusion.101 = (f32[24,196]{1,0:T(8,128)S(1)}, f32[24,196,768]{2,1,0:T(8,128)S(1)}) fusion(f32[196]{0:T(256)S(1)} %slice.68, bf16[24,768,384]{2,1,0:T(8,128)(2,1)} %get-tuple-element.114, f32[384,196]{0,1:T(8,128)S(1)} %copy-done.6, bf16[24,196,768]{2,0,1:T(8,128)(2,1)} %param.17), kind=kOutput, calls=%fused_computation.194 | convolution fusion | flops 2789053440 | bytes 36152464 | tf_op jit(solution)/shard_map/bck,ks->bsc/dot_general | solution.py:116
  130.2 13.9 %convert_reduce_fusion.6 = (u32[196,768]{1,0:T(8,128)S(1)}, u32[196,768]{1,0:T(8,128)S(1)}, f32[24,196,768]{2,1,0:T(8,128)}) fusion(f32[768]{0:T(1024)S(1)} %copy-done.17, f32[768,768]{1,0:T(8,128)S(1)} %copy-done.1, f32[24,196,768]{2,1,0:T(8,128)S(1)} %get-tuple-element.140, f32[768]{0:T(1024)S(1)} %get-tuple-element.90, f32[768]{0:T(1024)S(1)} %get-tuple-element.87, ...), kind=kOutput, calls=%fused_computation.57 | convolution fusion | flops 5610768384 | bytes 32511744 | tf_op jit(solution)/shard_map/bsc,ch->bsh/dot_general | solution.py:123
  144.1 36.3 %multiply_convert_fusion.1 = (bf16[24,196,768]{2,1,0:T(8,128)(2,1)}, f32[24,196,768]{2,1,0:T(8,128)}) fusion(f32[24,196,768]{2,1,0:T(8,128)} %get-tuple-element.141, f32[768]{0:T(1024)S(1)} %copy-done.17, u32[196,768]{1,0:T(8,128)S(1)} %get-tuple-element.83, u32[196,768]{1,0:T(8,128)S(1)} %get-tuple-element.82), kind=kLoop, calls=%fused_computation.66 | loop fusion | flops 249274368 | bytes 37334016 | tf_op jit(solution)/shard_map/convert_element_type | solution.py:125
  180.4 21.8 %convert_reduce_fusion.7 = (f32[768]{0:T(1024)}, bf16[24,196,768]{2,1,0:T(8,128)(2,1)S(1)}) fusion(f32[24,196,768]{2,1,0:T(8,128)} %get-tuple-element.113, f32[768,768]{1,0:T(8,128)S(1)} %copy-done.3, f32[24]{0:T(128)S(1)} %fusion.88, bf16[24,196,768]{2,0,1:T(8,128)(2,1)} %param.18, f32[24,196,768]{2,1,0:T(8,128)} %get-tuple-element.141, f32[768]{0:T(1024)S(1)} %copy-done.17), kind=kOutput, calls=%fused_computation.59 | convolution fusion | flops 5621906432 | bytes 45717600 | tf_op jit(solution)/shard_map/bsc,hc->bsh/dot_general | solution.py:134
  202.2 3.0 copy-done.28
  205.2 8.0 convolution_convert_fusion
  213.3 9.5 %convolution_convert_fusion.1 = bf16[24,196,768]{2,1,0:T(8,128)(2,1)S(1)} fusion(bf16[24,196,768]{2,1,0:T(8,128)(2,1)} %get-tuple-element.112, f32[768,768]{1,0:T(8,128)S(1)} %copy-done.3), kind=kOutput, calls=%fused_computation.84 | convolution fusion | flops 5553266688 | bytes 16809984 | tf_op jit(solution)/shard_map/bsh,hc->bsc/dot_general | solution.py:126
  222.9 4.4 copy.73
  232.1 12.8 %convolution_bitcast_fusion = f32[768,768]{1,0:T(8,128)} fusion(bf16[24,196,768]{2,1,0:T(8,128)(2,1)} %get-tuple-element.112, f32[24]{0:T(128)S(1)} %fusion.88, bf16[24,196,768]{2,0,1:T(8,128)(2,1)} %param.18), kind=kOutput, calls=%fused_computation.99 | convolution fusion | flops 5559902208 | bytes 16810080 | tf_op jit(solution)/shard_map/bsh,bsc->hc/dot_general | solution.py:133
  244.9 12.1 %convolution_bitcast_fusion.1 = f32[768,768]{1,0:T(8,128)} fusion(bf16[24,196,768]{2,1,0:T(8,128)(2,1)} %copy-done.28, f32[24,196,768]{2,1,0:T(8,128)S(1)} %bitcast.145, f32[768]{0:T(1024)S(1)} %get-tuple-element.90, f32[768]{0:T(1024)S(1)} %get-tuple-element.87, f32[24,196]{1,0:T(8,128)S(1)} %add_rsqrt_fusion, f32[24,196]{1,0:T(8,128)S(1)} %broadcast_multiply_fusion.4), kind=kOutput, calls=%fused_computation.100 | convolution fusion | flops 5567127552 | bytes 24079104 | tf_op jit(solution)/shard_map/bsc,bsh->ch/dot_general | solution.py:136
  257.0 96.3 %all-reduce.5.cloned.1.call-done = bf16[24,196,768]{2,1,0:T(8,128)(2,1)} async-done(((bf16[24,196,768]{2,1,0:T(8,128)(2,1)}), bf16[24,196,768]{2,1,0:T(8,128)(2,1)}) %all-reduce.5.cloned.1.call-update) | async-done | bytes 7225360 | tf_op jit(solution)/shard_map/psum | solution.py:144
  353.3 12.0 %fusion.29 = (f32[768]{0:T(1024)S(1)}, f32[24,196]{1,0:T(8,128)S(1)}, f32[24,196]{1,0:T(8,128)S(1)}, f32[768]{0:T(1024)S(1)}) fusion(bf16[24,196,768]{2,1,0:T(8,128)(2,1)} %all-reduce.5.cloned.1.call-done, f32[24,196,768]{2,1,0:T(8,128)} %copy-done, f32[24,196]{1,0:T(8,128)S(1)} %add_rsqrt_fusion, f32[24,196]{1,0:T(8,128)S(1)} %broadcast_multiply_fusion.4, ...), kind=kLoop, calls=%fused_computation.52 | loop fusion | flops 36115776 | bytes 21760512 | tf_op jit(solution)/shard_map/reduce_sum | solution.py:44
  366.5 164.7 %all-gather.3.cloned.1.call-done = bf16[96,196,768]{2,0,1:T(8,128)(2,1)} async-done(((bf16[24,196,768]{2,0,1:T(8,128)(2,1)}), bf16[96,196,768]{2,0,1:T(8,128)(2,1)}) %all-gather.3.cloned.1.call-update) | async-done | bytes 28901392 | tf_op jit(solution)/shard_map/all_gather | solution.py:16
  531.2 14.5 %reduce_sum.178 = bf16[24,196,768]{2,0,1:T(8,128)(2,1)} reduce(bf16[4,24,196,768]{3,1,0,2:T(8,128)(2,1)} %bitcast.148, bf16[]{:T(256)} %constant.73.clone.1), dimensions={0}, to_apply=%region_4.5 | reduce | flops 10838016 | bytes 36126720 | tf_op jit(solution)/shard_map/reduce_sum | solution.py:16
  545.7 24.5 %convert_reduce_fusion.8 = (f32[196]{0:T(256)}, f32[24,196,768]{2,1,0:T(8,128)}, bf16[24,196,768]{2,1,0:T(8,128)(2,1)}, f32[768]{0:T(1024)S(1)}) fusion(f32[24,196]{1,0:T(8,128)S(1)} %get-tuple-element.147, f32[24,196,768]{2,1,0:T(8,128)} %copy-done, f32[24,196]{1,0:T(8,128)S(1)} %broadcast_multiply_fusion.4, f32[24,196]{1,0:T(8,128)S(1)} %get-tuple-element.148, ...), kind=kLoop, calls=%fused_computation.60 | loop fusion | flops 75865152 | bytes 57888112 | tf_op jit(solution)/shard_map/reduce_sum | solution.py:51
  570.2 13.9 %convolution_bitcast_fusion.2 = f32[384,196]{0,1:T(8,128)} fusion(bf16[24,768,384]{2,1,0:T(8,128)(2,1)} %get-tuple-element.114, f32[24,196,768]{2,1,0:T(8,128)} %get-tuple-element.111), kind=kOutput, calls=%fused_computation.102 | convolution fusion | flops 2778144768 | bytes 28907520 | tf_op jit(solution)/shard_map/bck,bsc->ks/dot_general | solution.py:48
  584.2 30.6 %convert_reduce_fusion.2 = (f32[384]{0:T(512)}, bf16[24,768,384]{2,1,0:T(8,128)(2,1)}) fusion(f32[24,768,384]{2,1,0:T(8,128)} %get-tuple-element.115, f32[384,196]{0,1:T(8,128)S(1)} %copy-done.7, f32[24,196,768]{2,1,0:T(8,128)} %get-tuple-element.111, f32[24,768,384]{2,1,0:T(8,128)} %get-tuple-element.138, f32[384]{0:T(512)S(1)} %copy-done.23), kind=kOutput, calls=%fused_computation.7 | convolution fusion | flops 2898543616 | bytes 85533696 | tf_op jit(solution)/shard_map/bsc,ks->bck/dot_general | solution.py:52
  614.9 11.7 %fusion.45 = f32[196,384]{1,0:T(8,128)} fusion(bf16[24,768,384]{2,1,0:T(8,128)(2,1)} %get-tuple-element.144, f32[768]{0:T(1024)S(1)} %copy-done.27, f32[768]{0:T(1024)S(1)} %copy-done.21, f32[24,196]{1,0:T(8,128)S(1)} %copy-done.14, f32[24,196]{1,0:T(8,128)S(1)} %copy-done.12, bf16[24,196,768]{2,0,1:T(8,128)(2,1)} %param.17), kind=kOutput, calls=%fused_computation.101 | convolution fusion | flops 2796208128 | bytes 21725952 | tf_op jit(solution)/shard_map/bsc,bck->sk/dot_general | solution.py:56
  626.7 18.8 %fusion.22 = (f32[768]{0:T(1024)S(1)}, f32[24,196]{1,0:T(8,128)}, f32[24,196]{1,0:T(8,128)}, f32[24,768,196]{1,2,0:T(8,128)}) fusion(f32[24,196]{1,0:T(8,128)S(1)} %copy-done.14, f32[24,196]{1,0:T(8,128)S(1)} %copy-done.12, bf16[24,196,768]{2,0,1:T(8,128)(2,1)} %param.17, f32[768]{0:T(1024)S(1)} %copy-done.21, ...), kind=kOutput, calls=%fused_computation.45 | convolution fusion | flops 2807111424 | bytes 36214272 | tf_op jit(solution)/shard_map/bck,sk->bsc/dot_general | solution.py:58
  646.6 6.2 reduce_sum.186
  655.4 40.7 %all-reduce = (f32[5,768]{1,0:T(8,128)}, f32[580]{0:T(1024)}, f32[768]{0:T(1024)}) all-reduce(f32[5,768]{1,0:T(8,128)S(1)} %stack.86, f32[580]{0:T(1024)} %pad_maximum_fusion.7, f32[768]{0:T(1024)} %get-tuple-element.145), channel_id=1, replica_groups=mesh['dp'=8,'mp'=4] {'dp'}, use_global_device_ids=true, to_apply=%region_17.18 | all-reduce | flops 5188 | bytes 41504 | tf_op jit(solution)/shard_map/psum | solution.py:155
  701.6 16.6 %fusion.21 = bf16[24,196,768]{2,1,0:T(8,128)(2,1)} fusion(f32[24,196,768]{2,1,0:T(8,128)} %get-tuple-element.111, f32[24,768,196]{1,2,0:T(8,128)} %get-tuple-element.142, f32[24,196]{1,0:T(8,128)S(1)} %broadcast_multiply_fusion, f32[24,196]{1,0:T(8,128)S(1)} %broadcast_multiply_fusion.1, f32[768]{0:T(1024)} %copy-done.20, f32[24,196]{1,0:T(8,128)} %copy-done.13, ...), kind=kLoop, calls=%fused_computation.44 | loop fusion | flops 36126720 | bytes 43430400 | tf_op jit(solution)/shard_map/convert_element_type | solution.py:153
  718.3 7.6 copy.83
  725.8 4.4 copy.82
  731.5 83.8 %all-reduce.7.cloned.1.call-done = (f32[196,384]{1,0:T(8,128)}, f32[384,196]{0,1:T(8,128)}, f32[768,768]{1,0:T(8,128)}, f32[768,768]{1,0:T(8,128)}) async-done(((f32[196,384]{1,0:T(8,128)}, f32[384,196]{0,1:T(8,128)}, f32[768,768]{1,0:T(8,128)}, f32[768,768]{1,0:T(8,128)}), (f32[196,384]{1,0:T(8,128)}, f32[384,196]{0,1:T(8,128)}, f32[768,768]{1,0:T(8,128)}, ...) | async-done | bytes 5320720 | tf_op jit(solution)/shard_map/psum | solution.py:155
  822.1 6.9 fusion.53
  829.0 2.5 pad_maximum_fusion
  831.5 3.1 fusion.54
  (125 shorter events, 33.6 us)
Async XLA Ops:
  7.2 346.1 %all-reduce.5.cloned.1.call-start = ((), (), s32[]{:S(2)}) async-start(), calls=%async_computation | async-start | bytes 14745600 | tf_op jit(solution)/shard_map/psum | solution.py:144
  8.6 39.6 %copy-start.22 = (f32[384]{0:T(512)}, f32[384]{0:T(512)S(1)}, u32[]{:S(2)}) copy-start(f32[384]{0:T(512)S(1)} %slice.67) | copy-start | bytes 4612
  12.1 36.0 %copy-start.20 = (f32[768]{0:T(1024)}, f32[768]{0:T(1024)S(1)}, u32[]{:S(2)}) copy-start(f32[768]{0:T(1024)S(1)} %get-tuple-element.89) | copy-start | bytes 9220
  12.1 36.0 %copy-start.26 = (f32[768]{0:T(1024)}, f32[768]{0:T(1024)S(1)}, u32[]{:S(2)}) copy-start(f32[768]{0:T(1024)S(1)} %get-tuple-element.88) | copy-start | bytes 9220
  17.2 31.0 %copy-start.11 = (f32[24,196]{1,0:T(8,128)}, f32[24,196]{1,0:T(8,128)S(1)}, u32[]{:S(2)}) copy-start(f32[24,196]{1,0:T(8,128)S(1)} %broadcast_multiply_fusion.5) | copy-start | bytes 56452
  24.2 24.0 %copy-start.13 = (f32[24,196]{1,0:T(8,128)}, f32[24,196]{1,0:T(8,128)S(1)}, u32[]{:S(2)}) copy-start(f32[24,196]{1,0:T(8,128)S(1)} %add_rsqrt_fusion.1) | copy-start | bytes 56452
  48.2 67.2 %copy-start.6 = (f32[384,196]{0,1:T(8,128)S(1)}, f32[384,196]{0,1:T(8,128)}, u32[]{:S(2)}) copy-start(f32[384,196]{0,1:T(8,128)} %param.24) | copy-start | bytes 903172
  126.7 17.3 %copy-start = (f32[24,196,768]{2,1,0:T(8,128)}, f32[24,196,768]{2,1,0:T(8,128)S(1)}, u32[]{:S(2)}) copy-start(f32[24,196,768]{2,1,0:T(8,128)S(1)} %get-tuple-element.140) | copy-start | bytes 43352068
  144.1 36.3 %copy-start.3 = (f32[768,768]{1,0:T(8,128)S(1)}, f32[768,768]{1,0:T(8,128)}, u32[]{:S(2)}) copy-start(f32[768,768]{1,0:T(8,128)} %param.32) | copy-start | bytes 7077892
  180.4 24.8 %copy-start.2 = (f32[768,768]{1,0:T(8,128)S(1)}, f32[768,768]{1,0:T(8,128)}, u32[]{:S(2)}) copy-start(f32[768,768]{1,0:T(8,128)} %param.28) | copy-start | bytes 7077892
  213.3 317.9 %all-gather.3.cloned.1.call-start = ((), (), s32[]{:S(2)}) async-start(), calls=%async_computation.1 | async-start | bytes 36126720 | tf_op jit(solution)/shard_map/all_gather | solution.py:16
  227.4 587.9 %all-reduce.7.cloned.1.call-start = ((), (), s32[]{:S(2)}) async-start(), calls=%async_computation.2 | async-start | bytes 10665984 | tf_op jit(solution)/shard_map/psum | solution.py:155
  230.8 14.0 %slice-start = ((s8[14745600]{0:T(1024)(128)(4,1)}), s8[4194304]{0:T(1024)(128)(4,1)S(1)}, s32[]{:S(2)}) async-start(s8[14745600]{0:T(1024)(128)(4,1)} %bitcast.144), calls=%async_computation.3 | async-start | bytes 8388608
  232.1 12.8 %slice-start.1 = ((s8[14745600]{0:T(1024)(128)(4,1)}), s8[4194304]{0:T(1024)(128)(4,1)S(1)}, s32[]{:S(2)}) async-start(s8[14745600]{0:T(1024)(128)(4,1)} %bitcast.144), calls=%async_computation.4 | async-start | bytes 8388608
  232.1 12.8 %slice-start.2 = ((s8[14745600]{0:T(1024)(128)(4,1)}), s8[4194304]{0:T(1024)(128)(4,1)S(1)}, s32[]{:S(2)}) async-start(s8[14745600]{0:T(1024)(128)(4,1)} %bitcast.144), calls=%async_computation.5 | async-start | bytes 8388608
  232.1 12.8 %slice-start.3 = ((s8[14745600]{0:T(1024)(128)(4,1)}), s8[2162688]{0:T(1024)(128)(4,1)S(1)}, s32[]{:S(2)}) async-start(s8[14745600]{0:T(1024)(128)(4,1)} %bitcast.144), calls=%async_computation.6 | async-start | bytes 4325376
  531.2 14.5 %copy-start.19 = (f32[768]{0:T(1024)S(1)}, f32[768]{0:T(1024)}, u32[]{:S(2)}) copy-start(f32[768]{0:T(1024)} %get-tuple-element.86) | copy-start | bytes 9220
  570.2 13.9 %copy-start.7 = (f32[384,196]{0,1:T(8,128)S(1)}, f32[384,196]{0,1:T(8,128)}, u32[]{:S(2)}) copy-start(f32[384,196]{0,1:T(8,128)} %param.24) | copy-start | bytes 903172
  570.2 13.9 %copy-start.23 = (f32[384]{0:T(512)S(1)}, f32[384]{0:T(512)}, u32[]{:S(2)}) copy-start(f32[384]{0:T(512)} %copy-done.22) | copy-start | bytes 4612
  584.2 30.7 %copy-start.12 = (f32[24,196]{1,0:T(8,128)S(1)}, f32[24,196]{1,0:T(8,128)}, u32[]{:S(2)}) copy-start(f32[24,196]{1,0:T(8,128)} %copy-done.11) | copy-start | bytes 56452
  584.2 30.7 %copy-start.14 = (f32[24,196]{1,0:T(8,128)S(1)}, f32[24,196]{1,0:T(8,128)}, u32[]{:S(2)}) copy-start(f32[24,196]{1,0:T(8,128)} %copy-done.13) | copy-start | bytes 56452
  584.2 30.7 %copy-start.21 = (f32[768]{0:T(1024)S(1)}, f32[768]{0:T(1024)}, u32[]{:S(2)}) copy-start(f32[768]{0:T(1024)} %copy-done.20) | copy-start | bytes 9220
  584.2 30.7 %copy-start.27 = (f32[768]{0:T(1024)S(1)}, f32[768]{0:T(1024)}, u32[]{:S(2)}) copy-start(f32[768]{0:T(1024)} %copy-done.26) | copy-start | bytes 9220
  614.9 11.8 %copy-start.10 = (f32[196,384]{1,0:T(8,128)S(1)}, f32[196,384]{1,0:T(8,128)}, u32[]{:S(2)}) copy-start(f32[196,384]{1,0:T(8,128)} %param.22) | copy-start | bytes 903172
  645.4 50.6 %copy-start.15 = (f32[1,5,768]{2,0,1:T(1,128)S(1)}, f32[1,5,768]{2,0,1:T(1,128)}, u32[]{:S(2)}) copy-start(f32[1,5,768]{2,0,1:T(1,128)} %get-tuple-element.134) | copy-start | bytes 46084
  645.4 53.4 %copy-start.18 = (f32[768]{0:T(1024)S(1)}, f32[768]{0:T(1024)}, u32[]{:S(2)}) copy-start(f32[768]{0:T(1024)} %param.30) | copy-start | bytes 9220
  646.6 79.2 %slice-start.4 = ((s8[7372800]{0:T(1024)(128)(4,1)}), s8[3178496]{0:T(1024)(128)(4,1)S(1)}, s32[]{:S(2)}) async-start(s8[7372800]{0:T(1024)(128)(4,1)} %bitcast.146), calls=%async_computation.7 | async-start | bytes 6356992
  701.6 24.2 %slice-start.5 = ((s8[7372800]{0:T(1024)(128)(4,1)}), s8[4194304]{0:T(1024)(128)(4,1)S(1)}, s32[]{:S(2)}) async-start(s8[7372800]{0:T(1024)(128)(4,1)} %bitcast.146), calls=%async_computation.8 | async-start | bytes 8388608
  818.7 12.8 %slice-start.6 = ((s8[4718592]{0:T(1024)(128)(4,1)}), s8[4194304]{0:T(1024)(128)(4,1)S(1)}, s32[]{:S(2)}) async-start(s8[4718592]{0:T(1024)(128)(4,1)} %bitcast.149), calls=%async_computation.9 | async-start | bytes 8388608
  818.7 12.8 %copy-start.4 = (f32[768,768]{1,0:T(8,128)S(1)}, f32[768,768]{1,0:T(8,128)}, u32[]{:S(2)}) copy-start(f32[768,768]{1,0:T(8,128)} %param.32) | copy-start | bytes 7077892
  818.7 12.8 %copy-start.5 = (f32[768,768]{1,0:T(8,128)S(1)}, f32[768,768]{1,0:T(8,128)}, u32[]{:S(2)}) copy-start(f32[768,768]{1,0:T(8,128)} %get-tuple-element.103) | copy-start | bytes 7077892
  822.1 9.4 %slice-start.7 = ((s8[4718592]{0:T(1024)(128)(4,1)}), s8[524288]{0:T(1024)(128)(4,1)S(1)}, s32[]{:S(2)}) async-start(s8[4718592]{0:T(1024)(128)(4,1)} %bitcast.149), calls=%async_computation.10 | async-start | bytes 1048576
  (8 other events, 40.5 us)
Sparse Core Ops, SparseCore 0:
  213.4 139.8 all-reduce.4
  355.4 175.6 all-gather.2
  626.8 188.4 all-reduce.6
